TPU v7x, 512 devices: a whole 4x8x8 slice. The times are simulated.
512 devices in a mesh: segment: 32 (over y_lo, z), dp: 8 (over x, core), seq: 2 (over y_hi).
Axes of the slice: x: 4, y: 8 (y_hi: 2, y_lo: 4; y = y_hi * 4 + y_lo), z: 8, core: 2. Of those that a mesh axis runs over, the one named last changes fastest.
Arguments:
- stored_part_activation: bfloat16 [32, 2, 8, 256, 2048], P('segment', None, 'dp', 'seq'), may hold values from -64 to 64
- pending_sensitivity: bfloat16 [32, 8, 256, 2048], P('segment', 'dp', 'seq'), may hold values from -0.119628906 to 0.119628906
- uppermost_result_derivative: bfloat16 [1, 8, 256, 2048], P(None, 'dp', 'seq'), may hold values from -0.119628906 to 0.119628906
- scaling_factors: float32 [32, 4, 2048], P('segment'), may hold values from -0.5 to 5
- attended_tile_table: int32 [32, 2, 8, 2, 2], P('segment', None, 'dp'), may hold values from 0 to 1, as said below
- active_tile_number: int32 [32, 2, 8, 2], P('segment', None, 'dp'), may hold values from 1 to 2
Outputs:
- factor_derivatives: float32 [32, 4, 2048], P('segment')
Inputs may be any that keep to these rules, and one draw needn't show every extreme that they name: `attended_tile_table`: each list names every key block of its sample once; the allowed ones come first.
All inputs are finite; a program needn't handle non-finite values.
Results may differ from a plain program's by a relative error of at most 0.009.
Values may be sent and summed in bfloat16 or wider, within the bound.
A program may use at most 64 MiB of HBM per device.

v0:
```python
import jax
import jax.numpy as jnp
from jax import lax
from jax.sharding import PartitionSpec as P

HEAD_DIM = 128
BLK = 128
epsilon = 1e-06


def partner(block, axis, apart):
    count = lax.axis_size(axis)
    route = []
    for low in range(count):
        high = low | 1 << apart
        if high != low and high < count:
            route += [(low, high), (high, low)]
    return lax.ppermute(block, axis, route)


def from_behind(block, axis, distance):
    devices = range(lax.axis_size(axis))
    route = [(i - distance, i) for i in devices if i - distance in devices]
    return lax.ppermute(block, axis, route)


def normed_of(inputs):
    widened = inputs.astype(jnp.float32).reshape(
        inputs.shape[:-1] + (inputs.shape[-1] // HEAD_DIM, HEAD_DIM)
    )
    inv_rms = lax.rsqrt(jnp.mean(widened * widened, axis=-1, keepdims=True) + epsilon)
    return (widened * inv_rms, inv_rms)


def norm_back(grad_norm, norm_val, inv_rms):
    return inv_rms * (grad_norm - norm_val * jnp.mean(grad_norm * norm_val, axis=-1, keepdims=True))


def allowed_blocks(block_list, live_count):
    block_total = block_list.shape[0]
    live_slots = jnp.arange(block_total)[None, :] < live_count[:, None]
    matches = (block_list[:, :, None] == jnp.arange(block_total)[None, None, :]) & live_slots[
        :, :, None
    ]
    return jnp.any(matches, axis=1)


def token_mask(permitted, query_half, seq_index, dev_blocks):
    local_blocks = jnp.arange(dev_blocks, dtype=jnp.int32)
    query_rows = query_half * dev_blocks + local_blocks
    key_order = jnp.concatenate(
        [seq_index * dev_blocks + local_blocks, (1 - seq_index) * dev_blocks + local_blocks]
    )
    picked = permitted[query_rows[:, None], key_order[None, :]]
    return jnp.repeat(jnp.repeat(picked, BLK, axis=0), BLK, axis=1)


def attend(query_norm, key_norm, gain_heads, allowed, incoming, scaling):
    queries = (query_norm * gain_heads[0]).astype(jnp.bfloat16)
    key_mat = (key_norm * gain_heads[1]).astype(jnp.bfloat16)
    val_mat = (key_norm * gain_heads[2]).astype(jnp.bfloat16)
    scores = (
        jnp.einsum("thd,shd->hts", queries, key_mat, preferred_element_type=jnp.float32) * scaling
    )
    scores = jnp.where(allowed[None], scores, -jnp.inf)
    exped = jnp.exp(scores - jnp.max(scores, axis=-1, keepdims=True))
    probs = exped / jnp.sum(exped, axis=-1, keepdims=True)
    probs_low = probs.astype(jnp.bfloat16)
    output = jnp.einsum("hts,shd->thd", probs_low, val_mat, preferred_element_type=jnp.float32)
    grad_out = (gain_heads[3] * incoming).astype(jnp.bfloat16)
    grad_probs = jnp.einsum("thd,shd->hts", grad_out, val_mat, preferred_element_type=jnp.float32)
    grad_scores = (
        probs * (grad_probs - jnp.sum(probs * grad_probs, axis=-1, keepdims=True))
    ).astype(jnp.bfloat16)
    return (queries, key_mat, probs_low, output, grad_out, grad_scores)


def shards(
    stored_part_activation,
    pending_sensitivity,
    uppermost_result_derivative,
    scaling_factors,
    attended_tile_table,
    active_tile_number,
):
    segments = lax.axis_size("segment")
    segment_index = lax.axis_index("segment")
    seq_index = lax.axis_index("seq")
    window = stored_part_activation.shape[1]
    row_count = stored_part_activation.shape[3]
    channels = stored_part_activation.shape[4]
    head_count = channels // HEAD_DIM
    dev_blocks = row_count // BLK
    scaling = HEAD_DIM ** (-0.5)
    own_window = stored_part_activation[0, :, 0]
    gain_heads = scaling_factors[0].reshape(4, head_count, HEAD_DIM)
    incoming_sensitivity = pending_sensitivity[0, 0].astype(jnp.float32)
    totals = jnp.zeros((4, head_count, HEAD_DIM), jnp.float32)
    for step_index in range(window):
        own_rows = own_window[step_index]
        other_rows = partner(own_rows, "seq", 0)
        permitted = allowed_blocks(
            attended_tile_table[0, step_index, 0], active_tile_number[0, step_index, 0]
        )
        own_norm, own_inv = normed_of(own_rows)
        other_norm, other_inv = normed_of(other_rows)
        key_norm = jnp.concatenate([own_norm, other_norm], axis=0)
        incoming = incoming_sensitivity.reshape(row_count, head_count, HEAD_DIM)
        own_allowed = token_mask(permitted, seq_index, seq_index, dev_blocks)
        queries, key_mat, probs_low, output, grad_out, grad_scores = attend(
            own_norm, key_norm, gain_heads, own_allowed, incoming, scaling
        )
        grad_query = (
            jnp.einsum("hts,shd->thd", grad_scores, key_mat, preferred_element_type=jnp.float32)
            * scaling
        )
        grad_key = (
            jnp.einsum("hts,thd->shd", grad_scores, queries, preferred_element_type=jnp.float32)
            * scaling
        )
        grad_value = jnp.einsum(
            "hts,thd->shd", probs_low, grad_out, preferred_element_type=jnp.float32
        )
        key_part = grad_key * gain_heads[1] + grad_value * gain_heads[2]
        self_part = key_part[:row_count]
        key_terms = jnp.sum(grad_key * key_norm, axis=0)
        value_terms = jnp.sum(grad_value * key_norm, axis=0)
        if step_index < window - 1:
            lent = norm_back(key_part[row_count:], other_norm, other_inv).astype(jnp.bfloat16)
            returned = partner(lent, "seq", 0).astype(jnp.float32)
        grad_terms = jnp.stack(
            [
                jnp.sum(grad_query * own_norm, axis=0),
                key_terms,
                value_terms,
                jnp.sum(output * incoming, axis=0),
            ]
        )
        totals = totals + grad_terms
        if step_index < window - 1:
            grad_input = (
                incoming
                + norm_back(grad_query * gain_heads[0] + self_part, own_norm, own_inv)
                + returned
            )
            received = from_behind(grad_input.reshape(row_count, channels), "segment", -1)
            incoming_sensitivity = jnp.where(
                segment_index == segments - 1,
                uppermost_result_derivative[step_index, 0].astype(jnp.float32),
                received,
            )
    summed = lax.psum(totals.reshape(4, channels), ("dp", "seq"))
    return summed[None]


def solution(mesh):
    placed = (
        P("segment", None, "dp", "seq", None),
        P("segment", "dp", "seq", None),
        P(None, "dp", "seq", None),
        P("segment", None, None),
        P("segment", None, "dp", None, None),
        P("segment", None, "dp", None),
    )
    return jax.shard_map(
        shards, mesh=mesh, in_specs=placed, out_specs=P("segment", None, None), check_vma=False
    )
```

profile of v0, /device:TPU:24, one launch (start us, length us, event | category | flops | bytes accessed | tf_op | source)
XLA Modules:
  0.0 220.2 jit_solution(2187491883206557950)
XLA Ops:
  0.0 2.7 %slice_convert_fusion = (f32[1,1,1,128,2048]{4,3,2,1,0:T(8,128)}, bf16[128,2048]{1,0:T(8,128)(2,1)}, bf16[128,2048]{1,0:T(8,128)(2,1)}, f32[1,1,1,128,2048]{4,3,2,1,0:T(8,128)S(1)}) fusion(bf16[1,2,1,128,2048]{4,3,2,1,0:T(8,128)(2,1)} %param.6), kind=kLoop, calls=%fused_computation.75 | loop fusion | flops 524288 | bytes 4194304 | tf_op jit(solution)/shard_map/convert_element_type | solution.py:28
  2.7 5.0 %collective-permute-start = (bf16[128,2048]{1,0:T(8,128)(2,1)}, bf16[128,2048]{1,0:T(8,128)(2,1)}, u32[]{:S(2)}, u32[]{:S(2)}) collective-permute-start(bf16[128,2048]{1,0:T(8,128)(2,1)} %get-tuple-element.12), channel_id=1, source_target_pairs={{0,1},{1,0},{2,3},{3,2},{4,5},{5,4},{6,7},{7,6},{8,9},{9,8},{10,11... | collective-permute-start | bytes 1572872 | tf_op jit(solution)/shard_map/ppermute | solution.py:18
  7.8 4.7 %collective-permute-start.1 = (bf16[128,2048]{1,0:T(8,128)(2,1)}, bf16[128,2048]{1,0:T(8,128)(2,1)}, u32[]{:S(2)}, u32[]{:S(2)}) collective-permute-start(bf16[128,2048]{1,0:T(8,128)(2,1)} %get-tuple-element.13), channel_id=1, source_target_pairs={{0,1},{1,0},{2,3},{3,2},{4,5},{5,4},{6,7},{7,6},{8,9},{9,8},{10,11... | collective-permute-start | bytes 1572872 | tf_op jit(solution)/shard_map/ppermute | solution.py:18
  12.6 0.2 or_reduce_fusion
  12.9 0.1 and_reduce_fusion.1
  13.0 0.6 gather_fusion
  13.7 0.3 copy.49
  14.1 0.1 broadcast_multiply_fusion.3
  14.2 0.6 copy-done.11
  14.8 1.5 copy.58
  16.4 0.1 multiply_reduce_fusion.5
  16.5 0.1 and_reduce_fusion
  16.6 2.3 %copy.53 = f32[1,1,128,2048]{2,3,1,0:T(8,128)} copy(bf16[1,1,128,2048]{3,2,1,0:T(8,128)(2,1)} %param.7) | data formatting | bytes 1572864 | tf_op jit(solution)/shard_map/convert_element_type | solution.py:97
  18.9 0.6 gather_fusion.1
  19.5 1.1 broadcast_multiply_fusion.1
  20.6 12.6 %collective-permute-done = bf16[128,2048]{1,0:T(8,128)(2,1)} collective-permute-done((bf16[128,2048]{1,0:T(8,128)(2,1)}, bf16[128,2048]{1,0:T(8,128)(2,1)}, u32[]{:S(2)}, u32[]{:S(2)}) %collective-permute-start) | collective-permute-done | bytes 524320 | tf_op jit(solution)/shard_map/ppermute | solution.py:18
  33.2 1.2 copy.50
  34.5 1.1 broadcast_multiply_fusion.2
  35.6 3.9 %fusion.49 = (f32[16,128]{1,0:T(8,128)S(1)}, f32[16,128,256]{2,1,0:T(8,128)}) fusion(pred[256]{0:T(512)(128)(4,1)S(1)} %broadcast_bitcast_fusion.1, f32[16,128]{1,0:T(8,128)S(1)} %bitcast.124, f32[128,16,128]{0,2,1:T(8,128)} %broadcast_multiply_fusion.2, f32[128,16,128]{0,2,1:T(8,128)S(1)} %broadcast_multiply_fusion.3, f32[16,128]{1,0:T(8,128)S(1)} %bitcast.119), kind=kOutput, calls=%fused_computation.119 | convolution fusion | flops 138412288 | bytes 4219136 | tf_op jit(solution)/shard_map/sub | solution.py:66
  39.5 2.8 %fusion.26 = f32[16,128,256]{2,1,0:T(8,128)S(1)} fusion(f32[128,16,128]{0,2,1:T(8,128)} %bitcast.110, f32[16,128]{1,0:T(8,128)S(1)} %bitcast.141, f32[16,128,256]{2,1,0:T(8,128)} %get-tuple-element.24, f32[16,128]{1,0:T(8,128)S(1)} %get-tuple-element.23), kind=kOutput, calls=%fused_computation.70 | convolution fusion | flops 135790592 | bytes 5259264 | tf_op jit(solution)/shard_map/hts,thd->shd/dot_general | solution.py:121
  42.4 0.3 copy-done.5
  42.7 2.2 multiply_reduce_fusion.1
  44.9 0.7 multiply_convert_fusion.3
  45.6 1.9 fusion.5
  47.6 1.9 multiply_reduce_fusion.3
  49.5 1.0 multiply_convert_fusion.7
  50.5 6.3 %collective-permute-start.2 = (bf16[128,16,128]{0,2,1:T(8,128)(2,1)}, bf16[128,16,128]{0,2,1:T(8,128)(2,1)}, u32[]{:S(2)}, u32[]{:S(2)}) collective-permute-start(bf16[128,16,128]{0,2,1:T(8,128)(2,1)} %multiply_convert_fusion.7), channel_id=1, source_target_pairs={{0,1},{1,0},{2,3},{3,2},{4,5},{5,4},{6,7},{7,6},{8,9},{9,8},{10,11... | collective-permute-start | bytes 1572872 | tf_op jit(solution)/shard_map/ppermute | solution.py:18
  56.9 1.2 copy.59
  58.2 22.9 %collective-permute-done.2 = bf16[128,16,128]{0,2,1:T(8,128)(2,1)} collective-permute-done((bf16[128,16,128]{0,2,1:T(8,128)(2,1)}, bf16[128,16,128]{0,2,1:T(8,128)(2,1)}, u32[]{:S(2)}, u32[]{:S(2)}) %collective-permute-start.2) | collective-permute-done | bytes 524320 | tf_op jit(solution)/shard_map/ppermute | solution.py:18
  81.1 3.6 %convert_add_fusion = f32[128,16,128]{0,2,1:T(8,128)} fusion(bf16[128,16,128]{0,2,1:T(8,128)(2,1)} %collective-permute-done.2, f32[128,16,128]{0,2,1:T(8,128)} %bitcast.111, f32[128,16]{0,1:T(8,128)S(1)} %broadcast_multiply_fusion.7, f32[128,16]{0,1:T(8,128)S(1)} %add_rsqrt_fusion.3, f32[256,16,128]{0,2,1:T(8,128)} %copy-done.2, ...), kind=kLoop, calls=%fused_computation.45 | loop fusion | flops 2359296 | bytes 5791744 | tf_op jit(solution)/shard_map/add | solution.py:142
  84.7 2.6 %copy.62 = f32[128,2048]{1,0:T(8,128)} copy(f32[128,2048]{0,1:T(8,128)} %bitcast.114) | data formatting | bytes 2097152 | tf_op jit(solution)/shard_map/reshape | solution.py:146
  87.3 11.7 %collective-permute-start.3 = (f32[128,2048]{1,0:T(8,128)}, f32[128,2048]{1,0:T(8,128)}, u32[]{:S(2)}, u32[]{:S(2)}) collective-permute-start(f32[128,2048]{1,0:T(8,128)} %copy.62), channel_id=1, source_target_pairs={{16,0},{32,16},{48,32},{64,48},{80,64},{96,80},{112,96},{128,112},... | collective-permute-start | bytes 3145736 | tf_op jit(solution)/shard_map/ppermute | solution.py:24
  99.0 1.1 broadcast_multiply_fusion
  100.1 4.8 %fusion.50 = (f32[16,128]{1,0:T(8,128)S(1)}, f32[16,128,256]{2,1,0:T(8,128)}) fusion(pred[256]{0:T(512)(128)(4,1)S(1)} %broadcast_bitcast_fusion, f32[16,128]{1,0:T(8,128)S(1)} %bitcast.126, f32[128,16,128]{0,2,1:T(8,128)} %broadcast_multiply_fusion, f32[128,16,128]{0,2,1:T(8,128)} %broadcast_multiply_fusion.1, f32[16,128]{1,0:T(8,128)S(1)} %bitcast.121), kind=kOutput, calls=%fused_computation.120 | convolution fusion | flops 138412288 | bytes 4219136 | tf_op jit(solution)/shard_map/sub | solution.py:66
  104.9 2.6 %fusion.12 = f32[16,128]{1,0:T(8,128)S(1)} fusion(f32[128,16,128]{0,2,1:T(8,128)S(1)} %bitcast.113, f32[16,128]{1,0:T(8,128)S(1)} %bitcast.133, f32[128,16,128]{0,2,1:T(8,128)S(1)} %copy-done.1, f32[128,16,128]{0,2,1:T(8,128)S(1)} %broadcast_multiply_fusion.3, f32[16,128,256]{2,1,0:T(8,128)} %get-tuple-element.24, f32[16,128]{1,0:T(8,128)S(1)} %get-tuple-element.23), kind=kOutput, calls=%fused_computation.37 | convolution fusion | flops 137361408 | bytes 5267456 | tf_op jit(solution)/shard_map/hts,shd->thd/dot_general | solution.py:69
  107.5 14.2 %collective-permute-done.3 = f32[128,2048]{1,0:T(8,128)} collective-permute-done((f32[128,2048]{1,0:T(8,128)}, f32[128,2048]{1,0:T(8,128)}, u32[]{:S(2)}, u32[]{:S(2)}) %collective-permute-start.3) | collective-permute-done | bytes 1048608 | tf_op jit(solution)/shard_map/ppermute | solution.py:24
  121.7 1.3 convert_select_fusion
  123.1 1.3 copy.63
  124.4 3.4 %multiply_reduce_fusion = (f32[16,128]{1,0:T(8,128)S(1)}, f32[16,128,256]{2,1,0:T(8,128)S(1)}) fusion(f32[16,128,256]{2,1,0:T(8,128)S(1)} %copy-done.6, f32[16,128]{1,0:T(8,128)S(1)} %get-tuple-element.28, f32[16,128]{1,0:T(8,128)S(1)} %bitcast.134, f32[128,16,128]{0,2,1:T(8,128)} %broadcast_multiply_fusion, f32[128,16,128]{0,2,1:T(8,128)} %broadcast_multiply_fusion.1, ...), kind=kOutput, calls=%fused_computation.17 | convolution fusion | flops 137885696 | bytes 7372800 | tf_op jit(solution)/shard_map/thd,shd->hts/dot_general | solution.py:71
  127.8 0.8 multiply_convert_fusion
  128.6 0.4 copy-done.7
  129.0 0.3 copy-done.8
  129.4 0.7 fusion.13
  130.0 0.7 fusion.3
  130.7 0.5 copy-done.9
  131.3 1.1 fusion.2
  132.4 1.2 fusion.14
  133.7 86.5 %psum.7 = f32[1,4,2048]{2,1,0:T(4,128)} all-reduce(f32[1,4,2048]{2,1,0:T(4,128)S(1)} %fusion.32), channel_id=1, replica_groups=mesh['segment'=32,'dp'=8,'seq'=2] {'dp','seq'}, use_global_device_ids=true, to_apply=%region_22.23 | all-reduce | flops 8192 | bytes 65536 | tf_op jit(solution)/shard_map/psum | solution.py:152
  (44 shorter events, 0.8 us)
Async XLA Ops:
  0.0 12.8 %copy-start.13 = (s32[1,2,1,2]{3,2,1,0:T(1,128)S(1)}, s32[1,2,1,2]{3,2,1,0:T(1,128)}, u32[]{:S(2)}) copy-start(s32[1,2,1,2]{3,2,1,0:T(1,128)} %param.11) | copy-start | bytes 52
  0.0 12.8 %copy-start.12 = (s32[1,2,1,2,2]{4,3,2,1,0:T(2,128)S(1)}, s32[1,2,1,2,2]{4,3,2,1,0:T(2,128)}, u32[]{:S(2)}) copy-start(s32[1,2,1,2,2]{4,3,2,1,0:T(2,128)} %param.10) | copy-start | bytes 100
  2.7 30.5 %collective-permute-start = (bf16[128,2048]{1,0:T(8,128)(2,1)}, bf16[128,2048]{1,0:T(8,128)(2,1)}, u32[]{:S(2)}, u32[]{:S(2)}) collective-permute-start(bf16[128,2048]{1,0:T(8,128)(2,1)} %get-tuple-element.12), channel_id=1, source_target_pairs={{0,1},{1,0},{2,3},{3,2},{4,5},{5,4},{6,7},{7,6},{8,9},{9,8},{10,11... | collective-permute-start | bytes 1572872 | tf_op jit(solution)/shard_map/ppermute | solution.py:18
  7.8 49.1 %collective-permute-start.1 = (bf16[128,2048]{1,0:T(8,128)(2,1)}, bf16[128,2048]{1,0:T(8,128)(2,1)}, u32[]{:S(2)}, u32[]{:S(2)}) collective-permute-start(bf16[128,2048]{1,0:T(8,128)(2,1)} %get-tuple-element.13), channel_id=1, source_target_pairs={{0,1},{1,0},{2,3},{3,2},{4,5},{5,4},{6,7},{7,6},{8,9},{9,8},{10,11... | collective-permute-start | bytes 1572872 | tf_op jit(solution)/shard_map/ppermute | solution.py:18
  14.0 0.8 copy-start.11
  39.5 2.9 %copy-start = (f32[128,16,128]{0,2,1:T(8,128)S(1)}, f32[128,16,128]{0,2,1:T(8,128)}, u32[]{:S(2)}) copy-start(f32[128,16,128]{0,2,1:T(8,128)} %broadcast_multiply_fusion.2) | copy-start | bytes 3145732
  39.5 2.9 %copy-start.3 = (f32[1,1,128,2048]{2,3,1,0:T(8,128)S(1)}, f32[1,1,128,2048]{2,3,1,0:T(8,128)}, u32[]{:S(2)}) copy-start(f32[1,1,128,2048]{2,3,1,0:T(8,128)} %copy.53) | copy-start | bytes 3145732
  39.5 3.2 %copy-start.5 = (f32[16,128,256]{2,1,0:T(8,128)S(1)}, f32[16,128,256]{2,1,0:T(8,128)}, u32[]{:S(2)}) copy-start(f32[16,128,256]{2,1,0:T(8,128)} %get-tuple-element.24) | copy-start | bytes 6291460
  47.6 1.9 copy-start.2
  50.5 30.6 %collective-permute-start.2 = (bf16[128,16,128]{0,2,1:T(8,128)(2,1)}, bf16[128,16,128]{0,2,1:T(8,128)(2,1)}, u32[]{:S(2)}, u32[]{:S(2)}) collective-permute-start(bf16[128,16,128]{0,2,1:T(8,128)(2,1)} %multiply_convert_fusion.7), channel_id=1, source_target_pairs={{0,1},{1,0},{2,3},{3,2},{4,5},{5,4},{6,7},{7,6},{8,9},{9,8},{10,11... | collective-permute-start | bytes 1572872 | tf_op jit(solution)/shard_map/ppermute | solution.py:18
  87.3 34.4 %collective-permute-start.3 = (f32[128,2048]{1,0:T(8,128)}, f32[128,2048]{1,0:T(8,128)}, u32[]{:S(2)}, u32[]{:S(2)}) collective-permute-start(f32[128,2048]{1,0:T(8,128)} %copy.62), channel_id=1, source_target_pairs={{16,0},{32,16},{48,32},{64,48},{80,64},{96,80},{112,96},{128,112},... | collective-permute-start | bytes 3145736 | tf_op jit(solution)/shard_map/ppermute | solution.py:24
  100.1 4.8 %copy-start.1 = (f32[128,16,128]{0,2,1:T(8,128)S(1)}, f32[128,16,128]{0,2,1:T(8,128)}, u32[]{:S(2)}) copy-start(f32[128,16,128]{0,2,1:T(8,128)} %broadcast_multiply_fusion.2) | copy-start | bytes 3145732
  100.1 4.8 %copy-start.4 = (f32[1,1,128,2048]{2,3,1,0:T(8,128)S(1)}, f32[1,1,128,2048]{2,3,1,0:T(8,128)}, u32[]{:S(2)}) copy-start(f32[1,1,128,2048]{2,3,1,0:T(8,128)} %copy.53) | copy-start | bytes 3145732
  104.9 16.8 %copy-start.10 = (bf16[1,1,128,2048]{3,2,1,0:T(8,128)(2,1)S(1)}, bf16[1,1,128,2048]{3,2,1,0:T(8,128)(2,1)}, u32[]{:S(2)}) copy-start(bf16[1,1,128,2048]{3,2,1,0:T(8,128)(2,1)} %param.8) | copy-start | bytes 1572868
  107.5 16.9 %copy-start.6 = (f32[16,128,256]{2,1,0:T(8,128)S(1)}, f32[16,128,256]{2,1,0:T(8,128)}, u32[]{:S(2)}) copy-start(f32[16,128,256]{2,1,0:T(8,128)} %get-tuple-element.29) | copy-start | bytes 6291460
  127.8 1.2 copy-start.7
  127.8 1.5 copy-start.8
  130.0 1.2 copy-start.9
where the time goes:
time: 221 us; the launch traced here: 220 us
  blocking collectives  86.5 us (39%)
  waiting for transfers between devices  49.7 us (22%)
  starting transfers between devices  27.7 us (13%)
  matrix products  27.2 us (12%)
  other arithmetic  14.5 us (7%)
  local copies, waits for them, and re-layouts  14.3 us (6%)
    psum x1, blocking collectives, shards(): summed = lax.psum(totals.reshape(4, channels), ('dp', 'seq'))  86.5 us
    ppermute x3, waiting for transfers between devices, partner(): return lax.ppermute(block, axis, route)  35.5 us
    ppermute x3, starting transfers between devices, partner(): return lax.ppermute(block, axis, route)  16 us
    ppermute x1, waiting for transfers between devices, from_behind(): return lax.ppermute(block, axis, route)  14.2 us
    ppermute x1, starting transfers between devices, from_behind(): return lax.ppermute(block, axis, route)  11.7 us
    sub x2, matrix products, attend(): exped = jnp.exp(scores - jnp.max(scores, axis=-1, keepdims=True))  8.66 us
    dot_general x2, matrix products, attend(): jnp.einsum('thd,shd->hts', grad_out, val_mat, preferred_element_type=jnp....  5.55 us
  transfers between devices with their start and end apart: 4, of which 3 were waited for; matrix products, arithmetic and copies ran while one was open for 16% of the time, Pallas kernels for 0%

commit v1 on v0

--- a/solution.py
+++ b/solution.py
@@ -149,7 +149,9 @@
                 uppermost_result_derivative[step_index, 0].astype(jnp.float32),
                 received,
             )
-    summed = lax.psum(totals.reshape(4, channels), ("dp", "seq"))
+    summed = totals.reshape(4, channels)
+    for k in ("dp", "seq"):
+        summed = lax.psum(summed, axis_name=k)
     return summed[None]
 
 

time: 221 us -> 174 us (0.79)
  the two profiles are of different devices: /device:TPU:24 before, /device:TPU:56 now
where the time goes in v1:
time: 174 us; the launch traced here: 173 us
  waiting for transfers between devices  51 us (29%)
  blocking collectives  40.7 us (23%)
  matrix products  27.2 us (16%)
  starting transfers between devices  24.9 us (14%)
  other arithmetic  14.5 us (8%)
  local copies, waits for them, and re-layouts  14.3 us (8%)
    psum x2, blocking collectives, shards(): summed = lax.psum(summed, axis_name=k)  40.7 us
    ppermute x3, waiting for transfers between devices, partner(): return lax.ppermute(block, axis, route)  37.9 us
    ppermute x3, starting transfers between devices, partner(): return lax.ppermute(block, axis, route)  13.2 us
    ppermute x1, waiting for transfers between devices, from_behind(): return lax.ppermute(block, axis, route)  13.1 us
    ppermute x1, starting transfers between devices, from_behind(): return lax.ppermute(block, axis, route)  11.7 us
    sub x2, matrix products, attend(): exped = jnp.exp(scores - jnp.max(scores, axis=-1, keepdims=True))  8.66 us
    dot_general x2, matrix products, attend(): jnp.einsum('thd,shd->hts', grad_out, val_mat, preferred_element_type=jnp....  5.55 us
    dot_general x2, matrix products, shards(): jnp.einsum('hts,thd->shd', probs_low, grad_out, preferred_element_type=jn...  4 us
  transfers between devices with their start and end apart: 4, of which 3 were waited for; matrix products, arithmetic and copies ran while one was open for 20% of the time, Pallas kernels for 0%

profile of v1, /device:TPU:56, one launch (start us, length us, event | category | flops | bytes accessed | tf_op | source)
XLA Modules:
  0.0 172.8 jit_solution(13839083386566418701)
XLA Ops:
  0.0 2.7 %slice_convert_fusion = (f32[1,1,1,128,2048]{4,3,2,1,0:T(8,128)}, bf16[128,2048]{1,0:T(8,128)(2,1)}, bf16[128,2048]{1,0:T(8,128)(2,1)}, f32[1,1,1,128,2048]{4,3,2,1,0:T(8,128)S(1)}) fusion(bf16[1,2,1,128,2048]{4,3,2,1,0:T(8,128)(2,1)} %param.6), kind=kLoop, calls=%fused_computation.75 | loop fusion | flops 524288 | bytes 4194304 | tf_op jit(solution)/shard_map/convert_element_type | solution.py:28
  2.7 4.7 %collective-permute-start = (bf16[128,2048]{1,0:T(8,128)(2,1)}, bf16[128,2048]{1,0:T(8,128)(2,1)}, u32[]{:S(2)}, u32[]{:S(2)}) collective-permute-start(bf16[128,2048]{1,0:T(8,128)(2,1)} %get-tuple-element.12), channel_id=1, source_target_pairs={{0,1},{1,0},{2,3},{3,2},{4,5},{5,4},{6,7},{7,6},{8,9},{9,8},{10,11... | collective-permute-start | bytes 1572872 | tf_op jit(solution)/shard_map/ppermute | solution.py:18
  7.4 5.0 %collective-permute-start.1 = (bf16[128,2048]{1,0:T(8,128)(2,1)}, bf16[128,2048]{1,0:T(8,128)(2,1)}, u32[]{:S(2)}, u32[]{:S(2)}) collective-permute-start(bf16[128,2048]{1,0:T(8,128)(2,1)} %get-tuple-element.13), channel_id=1, source_target_pairs={{0,1},{1,0},{2,3},{3,2},{4,5},{5,4},{6,7},{7,6},{8,9},{9,8},{10,11... | collective-permute-start | bytes 1572872 | tf_op jit(solution)/shard_map/ppermute | solution.py:18
  12.6 0.2 or_reduce_fusion
  12.9 0.1 and_reduce_fusion.1
  13.0 0.6 gather_fusion
  13.7 0.3 copy.49
  14.1 0.1 broadcast_multiply_fusion.3
  14.2 0.6 copy-done.11
  14.8 1.5 copy.58
  16.5 0.1 and_reduce_fusion
  16.6 2.3 %copy.53 = f32[1,1,128,2048]{2,3,1,0:T(8,128)} copy(bf16[1,1,128,2048]{3,2,1,0:T(8,128)(2,1)} %param.7) | data formatting | bytes 1572864 | tf_op jit(solution)/shard_map/convert_element_type | solution.py:97
  18.9 0.6 gather_fusion.1
  19.5 1.1 broadcast_multiply_fusion.1
  20.6 13.8 %collective-permute-done = bf16[128,2048]{1,0:T(8,128)(2,1)} collective-permute-done((bf16[128,2048]{1,0:T(8,128)(2,1)}, bf16[128,2048]{1,0:T(8,128)(2,1)}, u32[]{:S(2)}, u32[]{:S(2)}) %collective-permute-start) | collective-permute-done | bytes 524320 | tf_op jit(solution)/shard_map/ppermute | solution.py:18
  34.4 1.2 copy.50
  35.8 1.1 broadcast_multiply_fusion.2
  36.9 3.9 %fusion.48 = (f32[16,128]{1,0:T(8,128)S(1)}, f32[16,128,256]{2,1,0:T(8,128)}) fusion(pred[256]{0:T(512)(128)(4,1)S(1)} %broadcast_bitcast_fusion.1, f32[16,128]{1,0:T(8,128)S(1)} %bitcast.124, f32[128,16,128]{0,2,1:T(8,128)} %broadcast_multiply_fusion.2, f32[128,16,128]{0,2,1:T(8,128)S(1)} %broadcast_multiply_fusion.3, f32[16,128]{1,0:T(8,128)S(1)} %bitcast.119), kind=kOutput, calls=%fused_computation.118 | convolution fusion | flops 138412288 | bytes 4219136 | tf_op jit(solution)/shard_map/sub | solution.py:66
  40.8 2.8 %fusion.26 = f32[16,128,256]{2,1,0:T(8,128)S(1)} fusion(f32[128,16,128]{0,2,1:T(8,128)} %bitcast.109, f32[16,128]{1,0:T(8,128)S(1)} %bitcast.141, f32[16,128,256]{2,1,0:T(8,128)} %get-tuple-element.24, f32[16,128]{1,0:T(8,128)S(1)} %get-tuple-element.23), kind=kOutput, calls=%fused_computation.70 | convolution fusion | flops 135790592 | bytes 5259264 | tf_op jit(solution)/shard_map/hts,thd->shd/dot_general | solution.py:121
  43.6 0.3 copy-done.5
  43.9 2.2 %multiply_reduce_fusion.1 = (f32[16,128]{1,0:T(8,128)S(1)}, f32[16,128,256]{2,1,0:T(8,128)S(1)}) fusion(f32[16,128,256]{2,1,0:T(8,128)S(1)} %copy-done.5, f32[16,128]{1,0:T(8,128)S(1)} %get-tuple-element.23, f32[16,128]{1,0:T(8,128)S(1)} %bitcast.131, f32[128,16,128]{0,2,1:T(8,128)S(1)} %copy-done, f32[128,16,128]{0,2,1:T(8,128)S(1)} %broadcast_multiply_fusion.3, ...), kind=kOutput, calls=%fused_computation.23 | convolution fusion | flops 137885696 | bytes 7372800 | tf_op jit(solution)/shard_map/thd,shd->hts/dot_general | solution.py:71
  46.1 0.7 multiply_convert_fusion.3
  46.9 1.9 %fusion.5 = (f32[16,128]{1,0:T(8,128)S(1)}, f32[16,128]{1,0:T(8,128)S(1)}, f32[256,16,128]{0,2,1:T(8,128)S(1)}) fusion(f32[128,16,128]{0,2,1:T(8,128)S(1)} %copy-done, f32[128,16,128]{0,2,1:T(8,128)S(1)} %broadcast_multiply_fusion.3, f32[16,128,256]{2,1,0:T(8,128)S(1)} %fusion.26, f32[16,128]{1,0:T(8,128)S(1)} %bitcast.132, ...), kind=kOutput, calls=%fused_computation.15 | convolution fusion | flops 139456512 | bytes 7380992 | tf_op jit(solution)/shard_map/hts,thd->shd/dot_general | solution.py:118
  48.8 1.9 %multiply_reduce_fusion.3 = (f32[128,16]{0,1:T(8,128)S(1)}, f32[128,16]{0,1:T(8,128)S(1)}, f32[16,128]{1,0:T(8,128)S(1)}, f32[16,128,128]{2,1,0:T(8,128)}) fusion(f32[128,16,128]{0,2,1:T(8,128)S(1)} %broadcast_multiply_fusion.3, f32[256,16,128]{0,2,1:T(8,128)S(1)} %get-tuple-element.10, f32[16,128]{1,0:T(8,128)S(1)} %broadcast_multiply_fusion.5, ...), kind=kOutput, calls=%fused_computation.48 | convolution fusion | flops 138143744 | bytes 8429568 | tf_op jit(solution)/shard_map/hts,shd->thd/dot_general | solution.py:114
  50.8 1.0 multiply_convert_fusion.7
  51.8 3.5 %collective-permute-start.2 = (bf16[128,16,128]{0,2,1:T(8,128)(2,1)}, bf16[128,16,128]{0,2,1:T(8,128)(2,1)}, u32[]{:S(2)}, u32[]{:S(2)}) collective-permute-start(bf16[128,16,128]{0,2,1:T(8,128)(2,1)} %multiply_convert_fusion.7), channel_id=1, source_target_pairs={{0,1},{1,0},{2,3},{3,2},{4,5},{5,4},{6,7},{7,6},{8,9},{9,8},{10,11... | collective-permute-start | bytes 1572872 | tf_op jit(solution)/shard_map/ppermute | solution.py:18
  55.3 1.2 copy.59
  56.7 24.1 %collective-permute-done.2 = bf16[128,16,128]{0,2,1:T(8,128)(2,1)} collective-permute-done((bf16[128,16,128]{0,2,1:T(8,128)(2,1)}, bf16[128,16,128]{0,2,1:T(8,128)(2,1)}, u32[]{:S(2)}, u32[]{:S(2)}) %collective-permute-start.2) | collective-permute-done | bytes 524320 | tf_op jit(solution)/shard_map/ppermute | solution.py:18
  80.7 3.6 %convert_add_fusion = f32[128,16,128]{0,2,1:T(8,128)} fusion(bf16[128,16,128]{0,2,1:T(8,128)(2,1)} %collective-permute-done.2, f32[128,16,128]{0,2,1:T(8,128)} %bitcast.110, f32[128,16]{0,1:T(8,128)S(1)} %broadcast_multiply_fusion.7, f32[128,16]{0,1:T(8,128)S(1)} %add_rsqrt_fusion.3, f32[256,16,128]{0,2,1:T(8,128)} %copy-done.2, ...), kind=kLoop, calls=%fused_computation.45 | loop fusion | flops 2359296 | bytes 5791744 | tf_op jit(solution)/shard_map/add | solution.py:142
  84.3 2.6 %copy.62 = f32[128,2048]{1,0:T(8,128)} copy(f32[128,2048]{0,1:T(8,128)} %bitcast.113) | data formatting | bytes 2097152 | tf_op jit(solution)/shard_map/reshape | solution.py:146
  86.9 11.7 %collective-permute-start.3 = (f32[128,2048]{1,0:T(8,128)}, f32[128,2048]{1,0:T(8,128)}, u32[]{:S(2)}, u32[]{:S(2)}) collective-permute-start(f32[128,2048]{1,0:T(8,128)} %copy.62), channel_id=1, source_target_pairs={{16,0},{32,16},{48,32},{64,48},{80,64},{96,80},{112,96},{128,112},... | collective-permute-start | bytes 3145736 | tf_op jit(solution)/shard_map/ppermute | solution.py:24
  98.6 1.1 broadcast_multiply_fusion
  99.7 4.8 %fusion.49 = (f32[16,128]{1,0:T(8,128)S(1)}, f32[16,128,256]{2,1,0:T(8,128)}) fusion(pred[256]{0:T(512)(128)(4,1)S(1)} %broadcast_bitcast_fusion, f32[16,128]{1,0:T(8,128)S(1)} %bitcast.126, f32[128,16,128]{0,2,1:T(8,128)} %broadcast_multiply_fusion, f32[128,16,128]{0,2,1:T(8,128)} %broadcast_multiply_fusion.1, f32[16,128]{1,0:T(8,128)S(1)} %bitcast.121), kind=kOutput, calls=%fused_computation.119 | convolution fusion | flops 138412288 | bytes 4219136 | tf_op jit(solution)/shard_map/sub | solution.py:66
  104.5 2.6 %fusion.12 = f32[16,128]{1,0:T(8,128)S(1)} fusion(f32[128,16,128]{0,2,1:T(8,128)S(1)} %bitcast.112, f32[16,128]{1,0:T(8,128)S(1)} %bitcast.133, f32[128,16,128]{0,2,1:T(8,128)S(1)} %copy-done.1, f32[128,16,128]{0,2,1:T(8,128)S(1)} %broadcast_multiply_fusion.3, f32[16,128,256]{2,1,0:T(8,128)} %get-tuple-element.24, f32[16,128]{1,0:T(8,128)S(1)} %get-tuple-element.23), kind=kOutput, calls=%fused_computation.37 | convolution fusion | flops 137361408 | bytes 5267456 | tf_op jit(solution)/shard_map/hts,shd->thd/dot_general | solution.py:69
  107.1 13.1 %collective-permute-done.3 = f32[128,2048]{1,0:T(8,128)} collective-permute-done((f32[128,2048]{1,0:T(8,128)}, f32[128,2048]{1,0:T(8,128)}, u32[]{:S(2)}, u32[]{:S(2)}) %collective-permute-start.3) | collective-permute-done | bytes 1048608 | tf_op jit(solution)/shard_map/ppermute | solution.py:24
  120.2 1.3 convert_select_fusion
  121.5 1.3 copy.63
  122.9 3.4 %multiply_reduce_fusion = (f32[16,128]{1,0:T(8,128)S(1)}, f32[16,128,256]{2,1,0:T(8,128)S(1)}) fusion(f32[16,128,256]{2,1,0:T(8,128)S(1)} %copy-done.6, f32[16,128]{1,0:T(8,128)S(1)} %get-tuple-element.28, f32[16,128]{1,0:T(8,128)S(1)} %bitcast.134, f32[128,16,128]{0,2,1:T(8,128)} %broadcast_multiply_fusion, f32[128,16,128]{0,2,1:T(8,128)} %broadcast_multiply_fusion.1, ...), kind=kOutput, calls=%fused_computation.17 | convolution fusion | flops 137885696 | bytes 7372800 | tf_op jit(solution)/shard_map/thd,shd->hts/dot_general | solution.py:71
  126.2 0.8 multiply_convert_fusion
  127.0 0.4 copy-done.7
  127.5 0.3 copy-done.8
  127.8 0.7 fusion.13
  128.5 0.7 fusion.3
  129.2 0.5 copy-done.9
  129.7 1.1 fusion.2
  130.8 1.2 fusion.14
  132.1 23.8 %psum.14 = f32[4,2048]{1,0:T(4,128)S(1)} all-reduce(f32[4,2048]{1,0:T(4,128)S(1)} %maximum_add_fusion), channel_id=1, replica_groups=mesh['segment'=32,'dp'=8,'seq'=2] {'dp'}, use_global_device_ids=true, to_apply=%region_22.23 | all-reduce | flops 8192 | bytes 65536 | tf_op jit(solution)/shard_map/psum | solution.py:154
  155.8 16.9 %psum.15 = f32[1,4,2048]{2,1,0:T(4,128)} all-reduce(f32[1,4,2048]{2,1,0:T(4,128)S(1)} %bitcast.117), channel_id=1, replica_groups=mesh['segment'=32,'dp'=8,'seq'=2] {'seq'}, use_global_device_ids=true, to_apply=%region_23.24 | all-reduce | flops 8192 | bytes 65536 | tf_op jit(solution)/shard_map/psum | solution.py:154
  (45 shorter events, 0.8 us)
Async XLA Ops:
  0.0 12.8 %copy-start.13 = (s32[1,2,1,2]{3,2,1,0:T(1,128)S(1)}, s32[1,2,1,2]{3,2,1,0:T(1,128)}, u32[]{:S(2)}) copy-start(s32[1,2,1,2]{3,2,1,0:T(1,128)} %param.11) | copy-start | bytes 52
  0.0 12.8 %copy-start.12 = (s32[1,2,1,2,2]{4,3,2,1,0:T(2,128)S(1)}, s32[1,2,1,2,2]{4,3,2,1,0:T(2,128)}, u32[]{:S(2)}) copy-start(s32[1,2,1,2,2]{4,3,2,1,0:T(2,128)} %param.10) | copy-start | bytes 100
  2.7 31.7 %collective-permute-start = (bf16[128,2048]{1,0:T(8,128)(2,1)}, bf16[128,2048]{1,0:T(8,128)(2,1)}, u32[]{:S(2)}, u32[]{:S(2)}) collective-permute-start(bf16[128,2048]{1,0:T(8,128)(2,1)} %get-tuple-element.12), channel_id=1, source_target_pairs={{0,1},{1,0},{2,3},{3,2},{4,5},{5,4},{6,7},{7,6},{8,9},{9,8},{10,11... | collective-permute-start | bytes 1572872 | tf_op jit(solution)/shard_map/ppermute | solution.py:18
  7.4 47.9 %collective-permute-start.1 = (bf16[128,2048]{1,0:T(8,128)(2,1)}, bf16[128,2048]{1,0:T(8,128)(2,1)}, u32[]{:S(2)}, u32[]{:S(2)}) collective-permute-start(bf16[128,2048]{1,0:T(8,128)(2,1)} %get-tuple-element.13), channel_id=1, source_target_pairs={{0,1},{1,0},{2,3},{3,2},{4,5},{5,4},{6,7},{7,6},{8,9},{9,8},{10,11... | collective-permute-start | bytes 1572872 | tf_op jit(solution)/shard_map/ppermute | solution.py:18
  14.0 0.8 copy-start.11
  40.8 2.9 %copy-start = (f32[128,16,128]{0,2,1:T(8,128)S(1)}, f32[128,16,128]{0,2,1:T(8,128)}, u32[]{:S(2)}) copy-start(f32[128,16,128]{0,2,1:T(8,128)} %broadcast_multiply_fusion.2) | copy-start | bytes 3145732
  40.8 2.9 %copy-start.3 = (f32[1,1,128,2048]{2,3,1,0:T(8,128)S(1)}, f32[1,1,128,2048]{2,3,1,0:T(8,128)}, u32[]{:S(2)}) copy-start(f32[1,1,128,2048]{2,3,1,0:T(8,128)} %copy.53) | copy-start | bytes 3145732
  40.8 3.2 %copy-start.5 = (f32[16,128,256]{2,1,0:T(8,128)S(1)}, f32[16,128,256]{2,1,0:T(8,128)}, u32[]{:S(2)}) copy-start(f32[16,128,256]{2,1,0:T(8,128)} %get-tuple-element.24) | copy-start | bytes 6291460
  48.8 1.9 %copy-start.2 = (f32[256,16,128]{0,2,1:T(8,128)}, f32[256,16,128]{0,2,1:T(8,128)S(1)}, u32[]{:S(2)}) copy-start(f32[256,16,128]{0,2,1:T(8,128)S(1)} %get-tuple-element.10) | copy-start | bytes 6291460
  51.8 29.0 %collective-permute-start.2 = (bf16[128,16,128]{0,2,1:T(8,128)(2,1)}, bf16[128,16,128]{0,2,1:T(8,128)(2,1)}, u32[]{:S(2)}, u32[]{:S(2)}) collective-permute-start(bf16[128,16,128]{0,2,1:T(8,128)(2,1)} %multiply_convert_fusion.7), channel_id=1, source_target_pairs={{0,1},{1,0},{2,3},{3,2},{4,5},{5,4},{6,7},{7,6},{8,9},{9,8},{10,11... | collective-permute-start | bytes 1572872 | tf_op jit(solution)/shard_map/ppermute | solution.py:18
  86.9 33.2 %collective-permute-start.3 = (f32[128,2048]{1,0:T(8,128)}, f32[128,2048]{1,0:T(8,128)}, u32[]{:S(2)}, u32[]{:S(2)}) collective-permute-start(f32[128,2048]{1,0:T(8,128)} %copy.62), channel_id=1, source_target_pairs={{16,0},{32,16},{48,32},{64,48},{80,64},{96,80},{112,96},{128,112},... | collective-permute-start | bytes 3145736 | tf_op jit(solution)/shard_map/ppermute | solution.py:24
  99.7 4.8 %copy-start.1 = (f32[128,16,128]{0,2,1:T(8,128)S(1)}, f32[128,16,128]{0,2,1:T(8,128)}, u32[]{:S(2)}) copy-start(f32[128,16,128]{0,2,1:T(8,128)} %broadcast_multiply_fusion.2) | copy-start | bytes 3145732
  99.7 4.8 %copy-start.4 = (f32[1,1,128,2048]{2,3,1,0:T(8,128)S(1)}, f32[1,1,128,2048]{2,3,1,0:T(8,128)}, u32[]{:S(2)}) copy-start(f32[1,1,128,2048]{2,3,1,0:T(8,128)} %copy.53) | copy-start | bytes 3145732
  104.5 15.7 %copy-start.10 = (bf16[1,1,128,2048]{3,2,1,0:T(8,128)(2,1)S(1)}, bf16[1,1,128,2048]{3,2,1,0:T(8,128)(2,1)}, u32[]{:S(2)}) copy-start(bf16[1,1,128,2048]{3,2,1,0:T(8,128)(2,1)} %param.8) | copy-start | bytes 1572868
  107.1 15.8 %copy-start.6 = (f32[16,128,256]{2,1,0:T(8,128)S(1)}, f32[16,128,256]{2,1,0:T(8,128)}, u32[]{:S(2)}) copy-start(f32[16,128,256]{2,1,0:T(8,128)} %get-tuple-element.29) | copy-start | bytes 6291460
  126.2 1.2 copy-start.7
  126.2 1.5 copy-start.8
  128.5 1.2 copy-start.9
